TPU v7x, 512 devices: a whole 4x8x8 slice. The times are simulated.
512 devices in a mesh: req: 32 (over x, z), tp: 16 (over y, core).
Axes of the slice: x: 4, y: 8, z: 8, core: 2. Of those that a mesh axis runs over, the one named last changes fastest.
Arguments:
- hidden: bfloat16 [32768, 2048], P(('req', 'tp')), may hold values from -6 to 6
- ln_gain: float32 [2048], replicated, may hold values from 0.1 to 1.9
- w_qkv: bfloat16 [2048, 3, 2048], P(None, None, 'tp'), may hold values from -0.125 to 0.125
- w_out: bfloat16 [2048, 2048], P('tp'), may hold values from -0.125 to 0.125
- cache_kv: bfloat16 [2, 512, 256, 2048], P(None, 'req', None, 'tp'), may hold values from -6 to 6
- cache_len: int32 [512], P('req'), may hold values from 16 to 256, as said below
- ancestors: int32 [512, 64, 64], P('req'), may hold values from 0 to 1, as said below
- accepted: int32 [512, 8], P('req'), may hold values from 0 to 14, as said below
Outputs:
- attn_proj: bfloat16 [32768, 2048], P(('req', 'tp'))
- kept_kv: bfloat16 [2, 512, 8, 2048], P(None, 'req', None, 'tp')
Inputs may be any that keep to these rules, and one draw needn't show every extreme that they name: `cache_len`: at least one request of the whole batch has exactly 256 cached positions. `ancestors`: entry (r, i, j) is 1 exactly where draft token j is token i or an ancestor of it in request r's tree; a token's parent has a lower index and token 0 is the root. `accepted`: each row holds, in increasing order, the first 8 tokens of a path down from the root of the request's tree, each entry the parent of the next.
All inputs are finite; a program needn't handle non-finite values.
Results may differ from a plain program's by a relative error of at most 0.018.
Values may be sent and summed in bfloat16 or wider, within the bound.
A program may use at most 64 MiB of HBM per device.

v0:
```python
import math

import jax
import jax.numpy as jnp
from jax import lax
from jax.sharding import PartitionSpec as P

HD = 128
KEY_BLOCK = 128


def block_part(queries, keys, values, positions, valid, slopes):
    heads = queries.shape[2]
    keys_four = keys.reshape(keys.shape[0], keys.shape[1], heads, HD)
    values_four = values.reshape(values.shape[0], values.shape[1], heads, HD)
    scores = jnp.einsum(
        "rihd,rjhd->rhij", queries, keys_four, preferred_element_type=jnp.float32
    ) * (1.0 / math.sqrt(HD))
    scores = scores + slopes[None, :, None, None] * positions[:, None, None, :]
    allowed = valid[:, None, :, :]
    scores = jnp.where(allowed, scores, -1e30)
    top = jnp.max(scores, axis=3)
    expo = jnp.where(allowed, jnp.exp(scores - top[..., None]), 0.0)
    total = jnp.sum(expo, axis=3)
    weights = expo.astype(jnp.bfloat16)
    summed = jnp.einsum("rhij,rjhd->rihd", weights, values_four, preferred_element_type=jnp.float32)
    return (top, total, summed)


def combine(first, second):
    top = jnp.maximum(first[0], second[0])
    scale_one = jnp.exp(first[0] - top)
    scale_two = jnp.exp(second[0] - top)
    total = first[1] * scale_one + second[1] * scale_two
    summed = (
        first[2] * jnp.transpose(scale_one, (0, 2, 1))[..., None]
        + second[2] * jnp.transpose(scale_two, (0, 2, 1))[..., None]
    )
    return (top, total, summed)


def cache_sweep(queries, keys, values, lengths, stride, slopes):
    requests, drafts, heads = (queries.shape[0], queries.shape[1], queries.shape[2])
    start_state = (
        jnp.full((requests, heads, drafts), -1e30, jnp.float32),
        jnp.zeros((requests, heads, drafts), jnp.float32),
        jnp.zeros((requests, drafts, heads, HD), jnp.float32),
    )
    count = keys.shape[1] // KEY_BLOCK

    def advance(block_index, state):
        start = block_index * KEY_BLOCK
        key_block = lax.dynamic_slice_in_dim(keys, start, KEY_BLOCK, 1)
        value_block = lax.dynamic_slice_in_dim(values, start, KEY_BLOCK, 1)
        cells = (start + jnp.arange(KEY_BLOCK)) * stride
        valid = (cells[None, :] < lengths[:, None])[:, None, :]
        positions = jnp.broadcast_to(cells.astype(jnp.float32)[None, :], (requests, KEY_BLOCK))
        return combine(state, block_part(queries, key_block, value_block, positions, valid, slopes))

    return lax.fori_loop(0, count, advance, start_state)


def on_device(hidden, ln_gain, w_qkv, w_out, cache_kv, cache_len, ancestors, accepted):
    values_f = hidden.astype(jnp.float32)
    mean = jnp.mean(values_f, axis=1, keepdims=True)
    centered = values_f - mean
    var = jnp.mean(centered * centered, axis=1, keepdims=True)
    normed = (centered * lax.rsqrt(var + 1e-05) * ln_gain[None, :]).astype(jnp.bfloat16)
    width = w_qkv.shape[2]
    heads = width // HD
    flat_weight = w_qkv.reshape(w_qkv.shape[0], 3 * width)
    joined = jnp.dot(
        lax.all_gather(normed, "tp", axis=0, tiled=True),
        flat_weight,
        preferred_element_type=jnp.float32,
    )
    requests = cache_len.shape[0]
    drafts = ancestors.shape[1]
    joined = joined.astype(jnp.bfloat16).reshape(requests, drafts, 3, heads, HD)
    queries = joined[:, :, 0]
    new_keys = joined[:, :, 1].reshape(requests, drafts, width)
    new_values = joined[:, :, 2].reshape(requests, drafts, width)
    head_ids = lax.axis_index("tp") * heads + jnp.arange(heads)
    all_heads = heads * lax.axis_size("tp")
    slopes = jnp.exp2(-8.0 * (head_ids.astype(jnp.float32) + 1.0) / all_heads)
    depth = jnp.sum(ancestors, axis=2) - 1
    draft_pos = (cache_len[:, None] + depth).astype(jnp.float32)
    draft_part = block_part(queries, new_keys, new_values, draft_pos, ancestors == 1, slopes)
    cache_part = cache_sweep(queries, cache_kv[0], cache_kv[1], cache_len, 1, slopes)
    merged = combine(cache_part, draft_part)
    attn = (merged[2] / jnp.transpose(merged[1], (0, 2, 1))[..., None]).astype(jnp.bfloat16)
    attn = attn.reshape(requests * drafts, width)
    attn_proj = lax.psum_scatter(
        jnp.dot(attn, w_out, preferred_element_type=jnp.float32).astype(jnp.bfloat16),
        "tp",
        scatter_dimension=0,
        tiled=True,
    )
    onehot = (accepted[:, :, None] == jnp.arange(drafts)[None, None, :]).astype(jnp.bfloat16)
    kept_keys = jnp.einsum("rad,rdc->rac", onehot, new_keys, preferred_element_type=jnp.float32)
    kept_values = jnp.einsum("rad,rdc->rac", onehot, new_values, preferred_element_type=jnp.float32)
    kept_kv = jnp.stack([kept_keys, kept_values]).astype(jnp.bfloat16)
    return (attn_proj, kept_kv)


def solution(mesh):
    placed = (
        P(("req", "tp"), None),
        P(),
        P(None, None, "tp"),
        P("tp", None),
        P(None, "req", None, "tp"),
        P("req"),
        P("req", None, None),
        P("req", None),
    )
    return jax.shard_map(
        on_device,
        mesh=mesh,
        in_specs=placed,
        out_specs=(P(("req", "tp"), None), P(None, "req", None, "tp")),
        check_vma=False,
    )
```

profile of v0, /device:TPU:1, one launch (start us, length us, event | category | flops | bytes accessed | tf_op | source)
XLA Modules:
  0.0 153.5 jit_solution(12655179019747754380)
XLA Ops:
  7.2 1.2 convert_reduce_fusion
  8.4 1.2 fusion.33
  9.6 1.8 %fusion.35 = bf16[64,2048]{1,0:T(8,128)(2,1)} fusion(bf16[64,2048]{1,0:T(8,128)(2,1)} %param.10, f32[2048]{0:T(1024)} %param.11, f32[64]{0:T(128)S(1)} %add_rsqrt_fusion, f32[64]{0:T(128)S(1)} %broadcast_multiply_fusion), kind=kLoop, calls=%fused_computation.56 | loop fusion | flops 655360 | bytes 532992 | tf_op jit(solution)/shard_map/convert_element_type | solution.py:68
  11.6 1.2 copy.18
  13.2 2.6 %copy.16 = bf16[2048,3,128]{0,2,1:T(8,128)(2,1)} copy(bf16[2048,3,128]{2,0,1:T(8,128)(2,1)} %param.12) | data formatting | bytes 3145728 | tf_op args[2]
  15.9 0.7 broadcast_compare_fusion.1
  16.7 2.7 %slice_bitcast_fusion = (bf16[16,256,128]{2,1,0:T(8,128)(2,1)S(1)}, bf16[16,256,128]{2,1,0:T(8,128)(2,1)}) fusion(bf16[2,16,256,128]{3,2,1,0:T(8,128)(2,1)} %param.14), kind=kLoop, calls=%fused_computation.48 | loop fusion | bytes 4194304 | tf_op jit(solution)/shard_map/squeeze | solution.py:89
  19.4 42.7 %all-gather.2.cloned.1.call-done = bf16[1024,2048]{1,0:T(8,128)(2,1)} async-done(((bf16[64,2048]{1,0:T(8,128)(2,1)}), bf16[1024,2048]{1,0:T(8,128)(2,1)}) %all-gather.2.cloned.1.call-update) | async-done | bytes 4194320 | tf_op jit(solution)/shard_map/all_gather | solution.py:73
  62.1 5.9 %convolution_convert_fusion.1 = bf16[1024,384]{1,0:T(8,128)(2,1)} fusion(bf16[1024,2048]{1,0:T(8,128)(2,1)} %all-gather.2.cloned.1.call-done, bf16[2048,384]{0,1:T(8,128)(2,1)} %bitcast.129), kind=kOutput, calls=%fused_computation.34 | convolution fusion | flops 1611005952 | bytes 6553600 | tf_op jit(solution)/shard_map/dot_general | solution.py:72
  68.0 2.4 %reshape.195 = bf16[16,64,3,1,128]{4,2,1,0,3:T(4,128)(2,1)S(1)} reshape(bf16[1024,384]{1,0:T(8,128)(2,1)} %convolution_convert_fusion.1) | data formatting | bytes 1572864 | tf_op jit(solution)/shard_map/reshape | solution.py:79
  70.4 2.2 %fusion.53 = (bf16[16,64,1,1,128]{4,2,1,0,3:T(2,128)(2,1)}, bf16[16,64,1,1,128]{4,2,1,0,3:T(2,128)(2,1)}, bf16[16,64,1,1,128]{4,2,1,0,3:T(2,128)(2,1)S(1)}) fusion(bf16[16,64,3,1,128]{4,2,1,0,3:T(4,128)(2,1)S(1)} %reshape.195), kind=kLoop, calls=%fused_computation.86 | loop fusion | bytes 1572864 | tf_op jit(solution)/shard_map/slice | solution.py:82
  72.7 0.8 copy-done.4
  73.5 5.6 %while.18 = (s32[]{:T(128)}, f32[16,1,64]{2,0,1:T(8,128)S(1)}, f32[16,1,64]{2,0,1:T(8,128)S(1)}, f32[16,64,1,128]{3,1,0,2:T(8,128)S(1)}, s32[16]{0:T(128)S(1)}, ...) while((s32[]{:T(128)}, f32[16,1,64]{2,0,1:T(8,128)S(1)}, ...), condition=%wide.region_5.6_spmd.clone, body=%wide.region_2.5_spmd.clone.sunk | while | flops 68954632 | bytes 4032779 | solution.py:60
  73.6 1.6 %fusion.68 = (f32[16,64]{1,0:T(8,128)S(1)}, f32[16,64,128]{2,1,0:T(8,128)S(1)}) fusion(f32[128]{0:T(128)S(1)} %convert_multiply_fusion.3, bf16[16,64,1,128]{3,1,0,2:T(8,128)(2,1)S(1)} %get-tuple-element.324, bf16[16,256,128]{2,1,0:T(8,128)(2,1)} %get-tuple-element.323, s32[]{:T(128)S(6)} %select_n.64, pred[16,128]{1,0:T(8,128)(4,1)S(1)} %broadcast_compare_fusion.3), kind=kOutput, calls=%fused_computation.85.clone.1 | convolution fusion | flops 34077696 | bytes 1317380 | tf_op jit(solution)/shard_map/while/body/eval_jaxpr/rihd,rjhd->rhij/dot_general | solution.py:16
  75.2 0.4 fusion.70
  75.6 0.6 fusion.72
  76.4 1.6 %fusion.68 = (f32[16,64]{1,0:T(8,128)S(1)}, f32[16,64,128]{2,1,0:T(8,128)S(1)}) fusion(f32[128]{0:T(128)S(1)} %convert_multiply_fusion.3, bf16[16,64,1,128]{3,1,0,2:T(8,128)(2,1)S(1)} %get-tuple-element.324, bf16[16,256,128]{2,1,0:T(8,128)(2,1)} %get-tuple-element.323, s32[]{:T(128)S(6)} %select_n.64, pred[16,128]{1,0:T(8,128)(4,1)S(1)} %broadcast_compare_fusion.3), kind=kOutput, calls=%fused_computation.85.clone.1 | convolution fusion | flops 34077696 | bytes 1317380 | tf_op jit(solution)/shard_map/while/body/eval_jaxpr/rihd,rjhd->rhij/dot_general | solution.py:16
  78.4 0.6 fusion.72
  79.1 1.6 %fusion.54 = (f32[16,64]{1,0:T(8,128)S(1)}, f32[16,64,64]{1,2,0:T(8,128)S(1)}) fusion(pred[16,64,64]{1,2,0:T(32,128)(4,1)} %broadcast_compare_fusion.1, f32[16,64]{1,0:T(8,128)S(1)} %convert_multiply_fusion.1, bf16[16,64,1,1,128]{4,2,1,0,3:T(2,128)(2,1)} %get-tuple-element.218, bf16[16,64,1,1,128]{4,2,1,0,3:T(2,128)(2,1)} %copy-done.4), kind=kOutput, calls=%fused_computation.87 | convolution fusion | flops 17038336 | bytes 860160 | tf_op jit(solution)/shard_map/rihd,rjhd->rhij/dot_general | solution.py:16
  80.8 0.6 fusion.28
  81.5 3.2 %convolution_convert_fusion = bf16[1024,2048]{1,0:T(8,128)(2,1)} fusion(bf16[1024,128]{1,0:T(8,128)(2,1)S(1)} %bitcast.130, bf16[128,2048]{1,0:T(8,128)(2,1)S(1)} %copy-done), kind=kOutput, calls=%fused_computation.33 | convolution fusion | flops 538968064 | bytes 4980736 | tf_op jit(solution)/shard_map/dot_general | solution.py:94
  84.7 0.7 copy-done.9
  86.2 0.6 pad_maximum_fusion
  86.9 59.8 %reduce-scatter.2.cloned.1.call-done = bf16[64,2048]{1,0:T(8,128)(2,1)} async-done(((bf16[1024,2048]{1,0:T(8,128)(2,1)}), bf16[64,2048]{1,0:T(8,128)(2,1)}) %reduce-scatter.2.cloned.1.call-update) | async-done | bytes 262160 | tf_op jit(solution)/shard_map/reduce_scatter | solution.py:93
  (48 shorter events, 2.3 us)
Async XLA Ops:
  7.2 74.3 %copy-start = (bf16[128,2048]{1,0:T(8,128)(2,1)S(1)}, bf16[128,2048]{1,0:T(8,128)(2,1)}, u32[]{:S(2)}) copy-start(bf16[128,2048]{1,0:T(8,128)(2,1)} %param.13) | copy-start | bytes 1572868
  7.2 5.6 %copy-start.3 = (s32[16,64,64]{2,1,0:T(8,128)S(1)}, s32[16,64,64]{2,1,0:T(8,128)}, u32[]{:S(2)}) copy-start(s32[16,64,64]{2,1,0:T(8,128)} %param.16) | copy-start | bytes 786436
  7.2 54.9 %all-gather.2.cloned.1.call-start = ((), (), s32[]{:S(2)}) async-start(), calls=%async_computation.1 | async-start | bytes 4456448 | tf_op jit(solution)/shard_map/all_gather | solution.py:73
  11.5 135.2 %reduce-scatter.2.cloned.1.call-start = ((), (), s32[]{:S(2)}) async-start(), calls=%async_computation.2 | async-start | bytes 4456448 | tf_op jit(solution)/shard_map/reduce_scatter | solution.py:93
  12.8 3.1 %copy-start.1 = (s32[16,64,64]{1,2,0:T(8,128)}, s32[16,64,64]{1,2,0:T(8,128)S(1)}, u32[]{:S(2)}) copy-start(s32[16,64,64]{1,2,0:T(8,128)S(1)} %copy.18) | copy-start | bytes 786436
  12.8 3.0 %copy-start.8 = (s32[16]{0:T(128)S(1)}, s32[16]{0:T(128)}, u32[]{:S(2)}) copy-start(s32[16]{0:T(128)} %param.15) | copy-start | bytes 196
  72.7 0.8 copy-start.4
  73.5 7.2 %copy-start.2 = (s32[16,64,64]{1,2,0:T(8,128)S(1)}, s32[16,64,64]{1,2,0:T(8,128)}, u32[]{:S(2)}) copy-start(s32[16,64,64]{1,2,0:T(8,128)} %copy-done.1) | copy-start | bytes 786436
  79.0 1.8 %copy-start.5 = (bf16[16,64,1,1,128]{4,2,1,0,3:T(2,128)(2,1)S(1)}, bf16[16,64,1,1,128]{4,2,1,0,3:T(2,128)(2,1)}, u32[]{:S(2)}) copy-start(bf16[16,64,1,1,128]{4,2,1,0,3:T(2,128)(2,1)} %get-tuple-element.217) | copy-start | bytes 786436
  79.0 1.8 %copy-start.7 = (pred[16,64,64]{1,2,0:T(32,128)(4,1)S(1)}, pred[16,64,64]{1,2,0:T(32,128)(4,1)}, u32[]{:S(2)}) copy-start(pred[16,64,64]{1,2,0:T(32,128)(4,1)} %broadcast_compare_fusion.1) | copy-start | bytes 196612
  84.7 0.7 copy-start.9
  84.7 1.1 copy-start.6
Sparse Core Ops, SparseCore 0:
  11.6 50.4 all-gather.1
  84.8 61.8 reduce-scatter.1
where the time goes:
time: 155 us; the launch traced here: 154 us
  waiting for transfers between devices  103 us (66%)
  matrix products  16.2 us (10%)
  between operations  14.3 us (9%)
  local copies, waits for them, and re-layouts  13.1 us (8%)
  other arithmetic  7.15 us (5%)
    reduce_scatter x1, waiting for transfers between devices, on_device(): lax.psum_scatter(jnp.dot(attn, w_out, preferred_element_type=jnp.float32)...  59.8 us
    all_gather x1, waiting for transfers between devices, on_device(): lax.all_gather(normed, 'tp', axis=0, tiled=True)  42.7 us
    dot_general x1, matrix products, on_device(): jnp.dot(lax.all_gather(normed, 'tp', axis=0, tiled=True), flat_weight, pr...  5.92 us
    unnamed x24, local copies, waits for them, and re-layouts  5.73 us
    dot_general x3, matrix products, block_part(): jnp.einsum('rihd,rjhd->rhij', queries, keys_four, preferred_element_type=...  4.81 us
    dot_general x1, matrix products, on_device(): jnp.dot(attn, w_out, preferred_element_type=jnp.float32)  3.18 us
  transfers between devices with their start and end apart: 2, of which 2 were waited for; matrix products, arithmetic and copies ran while one was open for 6% of the time, Pallas kernels for 0%

commit v1 on v0

v1 whole, which is shorter than its diff:
```python
import functools
import math

import jax
import jax.numpy as jnp
from jax import lax
from jax.experimental import pallas as pl
from jax.experimental.pallas import tpu as pltpu
from jax.sharding import PartitionSpec as P

HD = 128
CORES = 2
MESH = pl.DeviceIdType.MESH


class Ring:
    def __init__(self, n, me, device, slot, send, recv):
        self.n, self.me, self.device, self.slot = n, me, device, slot
        self.send, self.recv = send, recv
        self.far = n // 2
        self.sent = []

    def live(self, way, dist, h):
        return dist < self.far or (dist == self.far and h == way)

    def place(self, way, dist):
        step = self.n - dist if way == 0 else dist
        return lax.rem(self.me + step, self.n)

    def copy(self, way, dist, h):
        owner = self.me if dist == 1 else self.place(way, dist - 1)
        to = lax.rem(self.me + (1 if way == 0 else self.n - 1), self.n)
        ref = self.slot(owner, h)
        return pltpu.make_async_remote_copy(
            src_ref=ref,
            dst_ref=ref,
            send_sem=self.send.at[way, dist - 1, h],
            recv_sem=self.recv.at[way, dist - 1, h],
            device_id=self.device(to),
            device_id_type=MESH,
        )

    def start(self, way, dist, h):
        if self.live(way, dist, h):
            copy = self.copy(way, dist, h)
            copy.start()
            self.sent.append(copy)

    def own(self):
        for h in range(2):
            for way in range(2):
                self.start(way, 1, h)

    def step(self, dist, h, then=None):
        for way in range(2):
            if self.live(way, dist, h):
                ref = self.slot(self.place(way, dist), h)
                pltpu.make_async_remote_copy(
                    src_ref=ref,
                    dst_ref=ref,
                    send_sem=self.send.at[way, dist - 1, h],
                    recv_sem=self.recv.at[way, dist - 1, h],
                    device_id=self.device(lax.rem(self.me + 1, self.n)),
                    device_id_type=MESH,
                ).wait_recv()
                self.start(way, dist + 1, h)
                if then is not None:
                    then(way, dist, h)

    def events(self):
        return [(d, h) for d in range(1, self.far) for h in range(2)] + [(self.far, None)]

    def event(self, event, then=None):
        dist, h = event
        for half in (0, 1) if h is None else (h,):
            self.step(dist, half, then)

    def drain(self):
        for copy in self.sent:
            copy.wait_send()


def kernel(
    nx, nz, ny,
    hidden, gain, w_out, lens, accepted, w_qkv, cache, ancestors,
    out, kept,
    nbuf, wbuf, wq, kv, anc, asend, arecv, obuf, acc,
    local_sem, w_send, w_recv,
    y_send, y_recv, p_send, p_recv,
    xa_send, xa_recv, za_send, za_recv, zb_send, zb_recv, xb_send, xb_recv,
    a_send, a_recv, r_send, r_recv, o_send, o_recv,
):
    req, tp = lax.axis_index("req"), lax.axis_index("tp")
    x, z = lax.div(req, nz), lax.rem(req, nz)
    y, core = lax.div(tp, CORES), lax.rem(tp, CORES)
    ntp = ny * CORES
    half_heads = ntp // 2
    quarter = ntp // 4
    mate = (req, y * CORES + (1 - core))
    drafts, width = hidden.shape
    half_rows = drafts // 2
    half_width = width // CORES
    piece_rows, piece_cols = HD // nz, half_width // nx

    barrier = pltpu.get_barrier_semaphore()
    x_dev = lambda pos: (pos * nz + z, tp)
    z_dev = lambda pos: (x * nz + pos, tp)
    y_dev = lambda pos: (req, pos * CORES + core)
    peers = [(req, lax.rem(tp + o, ntp)) for o in range(1, ntp)]
    peers += [x_dev(lax.rem(x + s, nx)) for s in (1, nx - 1)]
    peers += [z_dev(lax.rem(z + s, nz)) for s in (1, nz - 1)]
    for peer in peers:
        pl.semaphore_signal(barrier, inc=1, device_id=peer, device_id_type=MESH)

    loads = [pltpu.make_async_copy(w_qkv.at[i], wq.at[:, pl.ds(i * HD, HD)], local_sem.at[i]) for i in range(3)]
    loads.append(pltpu.make_async_copy(cache, kv, local_sem.at[3]))
    loads.append(pltpu.make_async_copy(ancestors, anc, local_sem.at[4]))
    for load in loads:
        load.start()

    rows = hidden[...].astype(jnp.float32)
    mean = jnp.mean(rows, axis=1, keepdims=True)
    centered = rows - mean
    var = jnp.mean(centered * centered, axis=1, keepdims=True)
    normed = (centered * lax.rsqrt(var + 1e-05) * gain[...]).astype(jnp.bfloat16)
    nbuf[y, core, 0] = normed[:half_rows]
    nbuf[y, core, 1] = normed[half_rows:]

    pl.semaphore_wait(barrier, len(peers))

    def piece(c):
        return w_out.at[
            pl.ds(pl.multiple_of(z * piece_rows, piece_rows), piece_rows),
            pl.ds(pl.multiple_of(c * half_width + x * piece_cols, piece_cols), piece_cols),
        ]

    sends = []
    for o in range(1, ntp):
        to = lax.rem(tp + o, ntp)
        sends.append(pltpu.make_async_remote_copy(
            src_ref=piece(lax.rem(to, CORES)),
            dst_ref=wbuf.at[x, z, tp],
            send_sem=w_send.at[o],
            recv_sem=w_recv.at[o],
            device_id=(req, to),
            device_id_type=MESH,
        ))
        sends[-1].start()
    own_piece = pltpu.make_async_copy(piece(core), wbuf.at[x, z, tp], local_sem.at[5])
    own_piece.start()

    ring_y = Ring(ny, y, y_dev, lambda pos, h: nbuf.at[pos, core, h], y_send, y_recv)
    ring_y.own()

    def share(way, dist, h):
        owner = ring_y.place(way, dist) if dist else y
        copy = pltpu.make_async_remote_copy(
            src_ref=nbuf.at[owner, core, h],
            dst_ref=nbuf.at[owner, core, h],
            send_sem=p_send.at[way, dist, h],
            recv_sem=p_recv.at[way, dist, h],
            device_id=mate,
            device_id_type=MESH,
        )
        copy.start()
        sends.append(copy)

    def shared(way, dist, h):
        owner = ring_y.place(way, dist) if dist else y
        ref = nbuf.at[owner, 1 - core, h]
        pltpu.make_async_remote_copy(
            src_ref=ref, dst_ref=ref,
            send_sem=p_send.at[way, dist, h], recv_sem=p_recv.at[way, dist, h],
            device_id=mate, device_id_type=MESH,
        ).wait_recv()

    for h in range(2):
        share(0, 0, h)

    slope = jnp.exp2(jnp.full((1, HD), -8.0 / ntp, jnp.float32) * (tp + 1).astype(jnp.float32))[:, :1]
    scale = 1.0 / math.sqrt(HD)
    contract_last = (((1,), (1,)), ((), ()))

    def request(rid, q, k, v):
        length = lens[rid]
        mask = anc[rid]
        cells = kv.shape[2]
        depth = lax.dot_general(
            jnp.ones((8, drafts), jnp.bfloat16), mask.astype(jnp.float32).astype(jnp.bfloat16),
            contract_last, preferred_element_type=jnp.float32,
        )[:1] - 1.0
        cell = lax.broadcasted_iota(jnp.int32, (1, cells), 1)
        s_cache = lax.dot_general(q, kv[0, rid], contract_last, preferred_element_type=jnp.float32)
        s_cache = s_cache * scale + slope * cell.astype(jnp.float32)
        s_cache = jnp.where(cell < length, s_cache, -1e30)
        s_draft = lax.dot_general(q, k, contract_last, preferred_element_type=jnp.float32)
        s_draft = s_draft * scale + slope * (length.astype(jnp.float32) + depth)
        s_draft = jnp.where(mask == 1, s_draft, -1e30)
        top = jnp.maximum(jnp.max(s_cache, axis=1, keepdims=True), jnp.max(s_draft, axis=1, keepdims=True))
        e_cache = jnp.exp(s_cache - top)
        e_draft = jnp.exp(s_draft - top)
        total = jnp.sum(e_cache, axis=1, keepdims=True) + jnp.sum(e_draft, axis=1, keepdims=True)
        summed = jnp.dot(e_cache.astype(jnp.bfloat16), kv[1, rid], preferred_element_type=jnp.float32)
        summed += jnp.dot(e_draft.astype(jnp.bfloat16), v, preferred_element_type=jnp.float32)
        slots = kept.shape[2]
        slot = lax.broadcasted_iota(jnp.int32, (slots, drafts), 0)
        chosen = jnp.zeros((slots, drafts), jnp.int32)
        for a in range(slots):
            chosen = jnp.where(slot == a, accepted[a, rid], chosen)
        onehot = jnp.where(chosen == lax.broadcasted_iota(jnp.int32, (slots, drafts), 1), 1.0, 0.0).astype(jnp.bfloat16)
        kept[0, rid] = jnp.dot(onehot, k, preferred_element_type=jnp.float32).astype(jnp.bfloat16)
        kept[1, rid] = jnp.dot(onehot, v, preferred_element_type=jnp.float32).astype(jnp.bfloat16)
        return (summed / total).astype(jnp.bfloat16)

    order = []

    def attend(way, dist):
        if dist == 0:
            waits = [(0, 0, 0), (0, 0, 1)]
        elif dist < ring_y.far:
            waits = [(way, dist, 0), (way, dist, 1)]
        else:
            waits = [(0, dist, 0), (1, dist, 1)]
        for w in waits:
            shared(*w)
        owner = ring_y.place(way, dist) if dist else y
        tokens = nbuf[owner].reshape(CORES * drafts, width)
        joined = jnp.dot(tokens, wq[...], preferred_element_type=jnp.float32).astype(jnp.bfloat16)
        result = []
        for r in range(CORES):
            part = joined[r * drafts:(r + 1) * drafts]
            result.append(request(owner * CORES + r, part[:, :HD], part[:, HD:2 * HD], part[:, 2 * HD:]))
        result = jnp.concatenate(result, axis=0)
        if dist == 0:
            arecv[y, core] = result
            relay(0)
        else:
            offset = ny - dist if way == 0 else dist
            asend[offset] = result
            copy = pltpu.make_async_remote_copy(
                src_ref=asend.at[offset], dst_ref=arecv.at[y, core],
                send_sem=a_send.at[offset], recv_sem=a_recv.at[offset],
                device_id=y_dev(owner), device_id_type=MESH,
            )
            copy.start()
            sends.append(copy)
            order.append(offset)

    def source(offset):
        return lax.rem(y + ny - offset, ny) if offset else y

    def relay(offset):
        ref = arecv.at[source(offset), core]
        copy = pltpu.make_async_remote_copy(
            src_ref=ref, dst_ref=ref,
            send_sem=r_send.at[offset], recv_sem=r_recv.at[offset],
            device_id=mate, device_id_type=MESH,
        )
        copy.start()
        sends.append(copy)

    ring_xa = Ring(nx, x, x_dev, lambda pos, h: wbuf.at[pos, z, pl.ds(h * quarter, quarter)], xa_send, xa_recv)
    ring_za = Ring(nz, z, z_dev, lambda pos, h: wbuf.at[pl.ds(h * (nx // 2), nx // 2), pos, pl.ds(0, half_heads)], za_send, za_recv)
    ring_zb = Ring(nz, z, z_dev, lambda pos, h: wbuf.at[x, pos, pl.ds(half_heads + h * quarter, quarter)], zb_send, zb_recv)
    ring_xb = Ring(nx, x, x_dev, lambda pos, h: wbuf.at[pos, pl.ds(h * (nz // 2), nz // 2), pl.ds(half_heads, half_heads)], xb_send, xb_recv)

    own_piece.wait()
    for o in range(1, ntp):
        ref = wbuf.at[x, z, lax.rem(tp + ntp - o, ntp)]
        pltpu.make_async_remote_copy(
            src_ref=ref, dst_ref=ref, send_sem=w_send.at[o], recv_sem=w_recv.at[o],
            device_id=mate, device_id_type=MESH,
        ).wait_recv()
    ring_xa.own()
    ring_zb.own()
    for load in loads:
        load.wait()
    attend(0, 0)

    first = ring_zb.events()
    second_a = ring_za.events()
    second_b = ring_xb.events()
    pending = []
    for event in ring_xa.events():
        ring_xa.event(event)
    ring_za.own()
    for i, event in enumerate(ring_y.events()):
        ring_y.event(event, share)
        for _ in range(2):
            if first:
                ring_zb.event(first.pop(0))
                if not first:
                    ring_xb.own()
        if i and second_a:
            ring_za.event(second_a.pop(0))
        if not first and i >= 4 and second_b:
            ring_xb.event(second_b.pop(0))
        dist, h = event
        if h == 1:
            pending += [(0, dist), (1, dist)]
        elif h is None:
            pending.insert(0, (0, dist))
        if pending:
            attend(*pending.pop(0))
    while first:
        ring_zb.event(first.pop(0))
        if not first:
            ring_xb.own()
    while pending or second_a or second_b:
        if second_a:
            ring_za.event(second_a.pop(0))
        if second_b:
            ring_xb.event(second_b.pop(0))
        if pending:
            attend(*pending.pop(0))

    for offset in order:
        ref = arecv.at[source(offset), core]
        pltpu.make_async_remote_copy(
            src_ref=ref, dst_ref=ref, send_sem=a_send.at[offset], recv_sem=a_recv.at[offset],
            device_id=mate, device_id_type=MESH,
        ).wait_recv()
        relay(offset)

    for n, offset in enumerate([0] + order):
        chip = source(offset)
        ref = arecv.at[chip, 1 - core]
        pltpu.make_async_remote_copy(
            src_ref=ref, dst_ref=ref, send_sem=r_send.at[offset], recv_sem=r_recv.at[offset],
            device_id=mate, device_id_type=MESH,
        ).wait_recv()
        left = jnp.concatenate([arecv[chip, c] for c in range(CORES)], axis=1)
        for b in range(nx):
            right = jnp.concatenate(
                [wbuf[b, :, chip * CORES + c].reshape(HD, piece_cols) for c in range(CORES)], axis=0
            )
            columns = pl.ds(b * piece_cols, piece_cols)
            term = jnp.dot(left, right, preferred_element_type=jnp.float32)
            acc[:, columns] = term if n == 0 else acc[:, columns] + term

    for c in range(CORES):
        asend_rows = acc[c * drafts:(c + 1) * drafts].astype(jnp.bfloat16)
        obuf[c] = asend_rows
    last = pltpu.make_async_remote_copy(
        src_ref=obuf.at[1 - core], dst_ref=obuf.at[2], send_sem=o_send, recv_sem=o_recv,
        device_id=mate, device_id_type=MESH,
    )
    last.start()
    mine = pl.ds(pl.multiple_of(core * half_width, half_width), half_width)
    other = pl.ds(pl.multiple_of((1 - core) * half_width, half_width), half_width)
    out[:, mine] = obuf[core]
    last.wait()
    out[:, other] = obuf[2]
    for copy in sends:
        copy.wait_send()
    for ring in (ring_y, ring_xa, ring_za, ring_zb, ring_xb):
        ring.drain()


def on_device(nz, req_size, tp_size, hidden, ln_gain, w_qkv, w_out, cache_kv, cache_len, ancestors, accepted):
    nx, ny = req_size // nz, tp_size // CORES
    drafts, width = hidden.shape
    requests, slots = accepted.shape
    half_width = width // CORES
    bf16 = jnp.bfloat16
    dma = pltpu.SemaphoreType.DMA
    vmem = pl.BlockSpec(memory_space=pltpu.VMEM)
    smem = pl.BlockSpec(memory_space=pltpu.SMEM)
    hbm = pl.BlockSpec(memory_space=pl.ANY)
    ring = lambda n: [dma((2, n // 2, 2))] * 2
    out, kept = pl.pallas_call(
        functools.partial(kernel, nx, nz, ny),
        out_shape=(
            jax.ShapeDtypeStruct((drafts, width), bf16),
            jax.ShapeDtypeStruct((2, requests, slots, HD), bf16),
        ),
        in_specs=[vmem, vmem, vmem, smem, smem, hbm, hbm, hbm],
        out_specs=(vmem, vmem),
        scratch_shapes=[
            pltpu.VMEM((ny, CORES, 2, drafts // 2, width), bf16),
            pltpu.VMEM((nx, nz, tp_size, HD // nz, half_width // nx), bf16),
            pltpu.VMEM((width, 3 * HD), bf16),
            pltpu.VMEM(cache_kv.shape, bf16),
            pltpu.VMEM(ancestors.shape, jnp.int32),
            pltpu.VMEM((ny, CORES * drafts, HD), bf16),
            pltpu.VMEM((ny, CORES, CORES * drafts, HD), bf16),
            pltpu.VMEM((3, drafts, half_width), bf16),
            pltpu.VMEM((CORES * drafts, half_width), jnp.float32),
            dma((6,)),
            dma((tp_size,)),
            dma((tp_size,)),
            *ring(ny),
            dma((2, ny // 2 + 1, 2)),
            dma((2, ny // 2 + 1, 2)),
            *ring(nx), *ring(nz), *ring(nz), *ring(nx),
            dma((ny,)), dma((ny,)), dma((ny,)), dma((ny,)),
            dma, dma,
        ],
        compiler_params=pltpu.CompilerParams(
            collective_id=0, has_side_effects=True, vmem_limit_bytes=40 * 1024 * 1024
        ),
    )(
        hidden, ln_gain.reshape(1, width), w_out, cache_len, accepted.T,
        jnp.transpose(w_qkv, (1, 0, 2)), cache_kv, ancestors,
    )
    return (out, kept)


def solution(mesh, nz=8):
    placed = (
        P(("req", "tp"), None),
        P(),
        P(None, None, "tp"),
        P("tp", None),
        P(None, "req", None, "tp"),
        P("req"),
        P("req", None, None),
        P("req", None),
    )
    return jax.shard_map(
        functools.partial(on_device, nz, mesh.shape["req"], mesh.shape["tp"]),
        mesh=mesh,
        in_specs=placed,
        out_specs=(P(("req", "tp"), None), P(None, "req", None, "tp")),
        check_vma=False,
    )
```

time: 155 us -> 84.7 us (0.55)
  waiting for transfers between devices: 103 us -> 0 us
  Pallas kernels: 0 us -> 74.2 us
  matrix products: 16.2 us -> 0 us
  between operations: 14.3 us -> 0.66 us
  other arithmetic: 7.15 us -> 0 us
  local copies, waits for them, and re-layouts: 13.1 us -> 9.39 us
    pallas_call x0 -> x1, Pallas kernels: none -> 74.2 us  [on_device(): pl.pallas_call(functools.partial(kernel, nx, nz, ny), out_shape=(jax.Shap...]
    reduce_scatter x1 -> x0, waiting for transfers between devices: 59.8 us -> none  [on_device(): lax.psum_scatter(jnp.dot(attn, w_out, preferred_element_type=jnp.float32)...]
    all_gather x1 -> x0, waiting for transfers between devices: 42.7 us -> none  [on_device(): lax.all_gather(normed, 'tp', axis=0, tiled=True)]
    dot_general x10 -> x0, matrix products: 16.2 us -> none  [the longest x1 5.92 us: on_device(): jnp.dot(lax.all_gather(normed, 'tp', axis=0, tiled=True), flat_weight, pr...]
    unnamed x24 -> x18, local copies, waits for them, and re-layouts: 5.73 us -> 9.39 us
    reduce_sum x6 -> x0, other arithmetic: 3.64 us -> none  [the longest x1 1.19 us: on_device(): var = jnp.mean(centered * centered, axis=1, keepdims=True)]
    squeeze x1 -> x0, local copies, waits for them, and re-layouts: 2.71 us -> none  [on_device(): cache_kv[1]]
    reshape x1 -> x0, local copies, waits for them, and re-layouts: 2.4 us -> none  [on_device(): joined = joined.astype(jnp.bfloat16).reshape(requests, drafts, 3, heads, HD)]
  transfers between devices with their start and end apart: 2 -> 0, of which waited for: 2 -> 0; matrix products, arithmetic and copies ran while one was open for 6% -> 0% of each run, Pallas kernels for 0% -> 0%
where the time goes in v1:
time: 84.7 us; the launch traced here: 84.3 us
  Pallas kernels  74.2 us (88%)
  local copies, waits for them, and re-layouts  9.39 us (11%)
    pallas_call x1, Pallas kernels, on_device(): pl.pallas_call(functools.partial(kernel, nx, nz, ny), out_shape=(jax.Shap...  74.2 us
    unnamed x18, local copies, waits for them, and re-layouts  9.39 us

profile of v1, /device:TPU:1, one launch (start us, length us, event | category | flops | bytes accessed | tf_op | source)
XLA Modules:
  0.0 84.3 jit_solution(13904401980279914805)
XLA Ops:
  0.6 0.0 copy-start
  0.6 1.6 %copy-done = bf16[2,16,256,128]{3,2,1,0:T(8,128)(2,1)S(1)} copy-done((bf16[2,16,256,128]{3,2,1,0:T(8,128)(2,1)S(1)}, bf16[2,16,256,128]{3,2,1,0:T(8,128)(2,1)}, u32[]{:S(2)}) %copy-start) | copy-done | bytes 2097176
  2.2 0.0 copy-start.1
  2.2 1.4 %copy-done.1 = bf16[2048,3,128]{2,0,1:T(8,128)(2,1)S(1)} copy-done((bf16[2048,3,128]{2,0,1:T(8,128)(2,1)S(1)}, bf16[2048,3,128]{2,0,1:T(8,128)(2,1)}, u32[]{:S(2)}) %copy-start.1) | copy-done | bytes 1572888
  3.6 0.0 copy-start.2
  3.6 1.0 %copy-done.2 = bf16[128,2048]{1,0:T(8,128)(2,1)S(1)} copy-done((bf16[128,2048]{1,0:T(8,128)(2,1)S(1)}, bf16[128,2048]{1,0:T(8,128)(2,1)}, u32[]{:S(2)}) %copy-start.2) | copy-done | bytes 524312
  4.7 0.0 copy-start.3
  4.7 1.0 %copy-done.3 = s32[16,64,64]{2,1,0:T(8,128)S(1)} copy-done((s32[16,64,64]{2,1,0:T(8,128)S(1)}, s32[16,64,64]{2,1,0:T(8,128)}, u32[]{:S(2)}) %copy-start.3) | copy-done | bytes 262168
  5.7 0.0 copy-start.4
  5.7 0.9 %copy-done.4 = bf16[64,2048]{1,0:T(8,128)(2,1)S(1)} copy-done((bf16[64,2048]{1,0:T(8,128)(2,1)S(1)}, bf16[64,2048]{1,0:T(8,128)(2,1)}, u32[]{:S(2)}) %copy-start.4) | copy-done | bytes 262168
  6.7 0.0 copy-start.5
  6.7 0.7 copy-done.5
  7.4 0.0 copy-start.6
  7.4 0.7 copy-done.6
  8.1 0.0 copy-start.7
  8.1 0.7 copy-done.7
  8.7 74.2 %shard_map.95 = (bf16[64,2048]{1,0:T(8,128)(2,1)S(1)}, bf16[2,16,8,128]{3,2,1,0:T(8,128)(2,1)S(1)}) custom-call(bf16[64,2048]{1,0:T(8,128)(2,1)S(1)} %copy-done.4, f32[1,2048]{1,0:T(1,128)S(1)} %bitcast.4, bf16[128,2048]{1,0:T(8,128)(2,1)S(1)} %copy-done.2, s32[16]{0:T(128)S(1)} %copy-done.7, s32[8,16]{1,0:T(8,128)S(1)} %bitcast.5, ...), custom_call_target="tpu_custom_call" | custom-call | tf_op jit(solution)/shard_map/pallas_call | solution.py:371
  82.9 0.7 copy.12
  83.7 0.6 copy.13
Async XLA Ops:
  0.6 1.6 %copy-start = (bf16[2,16,256,128]{3,2,1,0:T(8,128)(2,1)S(1)}, bf16[2,16,256,128]{3,2,1,0:T(8,128)(2,1)}, u32[]{:S(2)}) copy-start(bf16[2,16,256,128]{3,2,1,0:T(8,128)(2,1)} %cache.1) | copy-start | bytes 6291460
  2.2 1.4 %copy-start.1 = (bf16[2048,3,128]{2,0,1:T(8,128)(2,1)S(1)}, bf16[2048,3,128]{2,0,1:T(8,128)(2,1)}, u32[]{:S(2)}) copy-start(bf16[2048,3,128]{2,0,1:T(8,128)(2,1)} %param.10) | copy-start | bytes 4718596
  3.6 1.0 %copy-start.2 = (bf16[128,2048]{1,0:T(8,128)(2,1)S(1)}, bf16[128,2048]{1,0:T(8,128)(2,1)}, u32[]{:S(2)}) copy-start(bf16[128,2048]{1,0:T(8,128)(2,1)} %w_out.1) | copy-start | bytes 1572868
  4.7 1.0 %copy-start.3 = (s32[16,64,64]{2,1,0:T(8,128)S(1)}, s32[16,64,64]{2,1,0:T(8,128)}, u32[]{:S(2)}) copy-start(s32[16,64,64]{2,1,0:T(8,128)} %ancestors.1) | copy-start | bytes 786436
  5.7 0.9 %copy-start.4 = (bf16[64,2048]{1,0:T(8,128)(2,1)S(1)}, bf16[64,2048]{1,0:T(8,128)(2,1)}, u32[]{:S(2)}) copy-start(bf16[64,2048]{1,0:T(8,128)(2,1)} %hidden.1) | copy-start | bytes 786436
  6.7 0.7 copy-start.5
  7.4 0.7 copy-start.6
  8.1 0.7 copy-start.7

commit v2 on v1

--- a/solution.py
+++ b/solution.py
@@ -82,12 +82,12 @@
 
 def kernel(
     nx, nz, ny,
-    hidden, gain, w_out, lens, accepted, w_qkv, cache, ancestors,
+    hidden_hbm, gain_hbm, w_out_hbm, lens_hbm, accepted_hbm, w_qkv, cache, ancestors,
     out, kept,
-    nbuf, wbuf, wq, kv, anc, asend, arecv, obuf, acc,
+    hidden, gain, w_out, lens, accepted, nbuf, wlow, whigh, wq, kv, anc, asend, arecv, obuf, acc,
     local_sem, w_send, w_recv,
     y_send, y_recv, p_send, p_recv,
-    xa_send, xa_recv, za_send, za_recv, zb_send, zb_recv, xb_send, xb_recv,
+    z_send, z_recv, x_send, x_recv,
     a_send, a_recv, r_send, r_recv, o_send, o_recv,
 ):
     req, tp = lax.axis_index("req"), lax.axis_index("tp")
@@ -109,15 +109,25 @@
     peers = [(req, lax.rem(tp + o, ntp)) for o in range(1, ntp)]
     peers += [x_dev(lax.rem(x + s, nx)) for s in (1, nx - 1)]
     peers += [z_dev(lax.rem(z + s, nz)) for s in (1, nz - 1)]
+    early = [
+        pltpu.make_async_copy(src, dst, local_sem.at[6 + i])
+        for i, (src, dst) in enumerate(((hidden_hbm, hidden), (gain_hbm, gain), (w_out_hbm, w_out)))
+    ]
+    for load in early:
+        load.start()
     for peer in peers:
         pl.semaphore_signal(barrier, inc=1, device_id=peer, device_id_type=MESH)
 
     loads = [pltpu.make_async_copy(w_qkv.at[i], wq.at[:, pl.ds(i * HD, HD)], local_sem.at[i]) for i in range(3)]
     loads.append(pltpu.make_async_copy(cache, kv, local_sem.at[3]))
     loads.append(pltpu.make_async_copy(ancestors, anc, local_sem.at[4]))
+    loads.append(pltpu.make_async_copy(lens_hbm, lens, local_sem.at[9]))
+    loads.append(pltpu.make_async_copy(accepted_hbm, accepted, local_sem.at[10]))
     for load in loads:
         load.start()
 
+    early[0].wait()
+    early[1].wait()
     rows = hidden[...].astype(jnp.float32)
     mean = jnp.mean(rows, axis=1, keepdims=True)
     centered = rows - mean
@@ -126,28 +136,49 @@
     nbuf[y, core, 0] = normed[:half_rows]
     nbuf[y, core, 1] = normed[half_rows:]
 
+    early[2].wait()
     pl.semaphore_wait(barrier, len(peers))
 
-    def piece(c):
+    def low_piece(c):
         return w_out.at[
             pl.ds(pl.multiple_of(z * piece_rows, piece_rows), piece_rows),
-            pl.ds(pl.multiple_of(c * half_width + x * piece_cols, piece_cols), piece_cols),
+            pl.ds(pl.multiple_of(c * half_width, half_width), half_width),
         ]
 
+    def high_piece(c):
+        return w_out.at[:, pl.ds(pl.multiple_of(c * half_width + x * piece_cols, piece_cols), piece_cols)]
+
+    def low_slot(head):
+        return wlow.at[z, head]
+
+    def high_slot(head):
+        return whigh.at[x, head - half_heads]
+
     sends = []
-    for o in range(1, ntp):
-        to = lax.rem(tp + o, ntp)
-        sends.append(pltpu.make_async_remote_copy(
-            src_ref=piece(lax.rem(to, CORES)),
-            dst_ref=wbuf.at[x, z, tp],
-            send_sem=w_send.at[o],
-            recv_sem=w_recv.at[o],
-            device_id=(req, to),
-            device_id_type=MESH,
-        ))
-        sends[-1].start()
-    own_piece = pltpu.make_async_copy(piece(core), wbuf.at[x, z, tp], local_sem.at[5])
-    own_piece.start()
+    kinds = ((tp < half_heads, low_piece, low_slot), (tp >= half_heads, high_piece, high_slot))
+
+    def spread(finish):
+        for mine_kind, part, slot in kinds:
+            @pl.when(mine_kind)
+            def _(part=part, slot=slot):
+                kept_piece = pltpu.make_async_copy(part(core), slot(tp), local_sem.at[5])
+                if finish:
+                    kept_piece.wait()
+                else:
+                    kept_piece.start()
+                for o in range(1, ntp):
+                    to = lax.rem(tp + o, ntp)
+                    copy = pltpu.make_async_remote_copy(
+                        src_ref=part(lax.rem(to, CORES)), dst_ref=slot(tp),
+                        send_sem=w_send.at[o], recv_sem=w_recv.at[tp],
+                        device_id=(req, to), device_id_type=MESH,
+                    )
+                    if finish:
+                        copy.wait_send()
+                    else:
+                        copy.start()
+
+    spread(False)
 
     ring_y = Ring(ny, y, y_dev, lambda pos, h: nbuf.at[pos, core, h], y_send, y_recv)
     ring_y.own()
@@ -259,42 +290,33 @@
         copy.start()
         sends.append(copy)
 
-    ring_xa = Ring(nx, x, x_dev, lambda pos, h: wbuf.at[pos, z, pl.ds(h * quarter, quarter)], xa_send, xa_recv)
-    ring_za = Ring(nz, z, z_dev, lambda pos, h: wbuf.at[pl.ds(h * (nx // 2), nx // 2), pos, pl.ds(0, half_heads)], za_send, za_recv)
-    ring_zb = Ring(nz, z, z_dev, lambda pos, h: wbuf.at[x, pos, pl.ds(half_heads + h * quarter, quarter)], zb_send, zb_recv)
-    ring_xb = Ring(nx, x, x_dev, lambda pos, h: wbuf.at[pos, pl.ds(h * (nz // 2), nz // 2), pl.ds(half_heads, half_heads)], xb_send, xb_recv)
-
-    own_piece.wait()
-    for o in range(1, ntp):
-        ref = wbuf.at[x, z, lax.rem(tp + ntp - o, ntp)]
-        pltpu.make_async_remote_copy(
-            src_ref=ref, dst_ref=ref, send_sem=w_send.at[o], recv_sem=w_recv.at[o],
-            device_id=mate, device_id_type=MESH,
-        ).wait_recv()
-    ring_xa.own()
-    ring_zb.own()
+    ring_z = Ring(nz, z, z_dev, lambda pos, h: wlow.at[pos, pl.ds(h * quarter, quarter)], z_send, z_recv)
+    ring_x = Ring(nx, x, x_dev, lambda pos, h: whigh.at[pos, pl.ds(h * quarter, quarter)], x_send, x_recv)
+
     for load in loads:
         load.wait()
     attend(0, 0)
 
-    first = ring_zb.events()
-    second_a = ring_za.events()
-    second_b = ring_xb.events()
+    spread(True)
+    for head in range(ntp):
+        @pl.when(tp != head)
+        def _(head=head):
+            ref = low_slot(head) if head < half_heads else high_slot(head)
+            pltpu.make_async_remote_copy(
+                src_ref=ref, dst_ref=ref, send_sem=w_send.at[0], recv_sem=w_recv.at[head],
+                device_id=mate, device_id_type=MESH,
+            ).wait_recv()
+    ring_z.own()
+    ring_x.own()
+
+    along_z, along_x = ring_z.events(), ring_x.events()
     pending = []
-    for event in ring_xa.events():
-        ring_xa.event(event)
-    ring_za.own()
     for i, event in enumerate(ring_y.events()):
         ring_y.event(event, share)
-        for _ in range(2):
-            if first:
-                ring_zb.event(first.pop(0))
-                if not first:
-                    ring_xb.own()
-        if i and second_a:
-            ring_za.event(second_a.pop(0))
-        if not first and i >= 4 and second_b:
-            ring_xb.event(second_b.pop(0))
+        if i:
+            ring_z.event(along_z.pop(0))
+        if i % 2 == 0 and i:
+            ring_x.event(along_x.pop(0))
         dist, h = event
         if h == 1:
             pending += [(0, dist), (1, dist)]
@@ -302,15 +324,11 @@
             pending.insert(0, (0, dist))
         if pending:
             attend(*pending.pop(0))
-    while first:
-        ring_zb.event(first.pop(0))
-        if not first:
-            ring_xb.own()
-    while pending or second_a or second_b:
-        if second_a:
-            ring_za.event(second_a.pop(0))
-        if second_b:
-            ring_xb.event(second_b.pop(0))
+    while pending or along_z or along_x:
+        if along_z:
+            ring_z.event(along_z.pop(0))
+        if along_x:
+            ring_x.event(along_x.pop(0))
         if pending:
             attend(*pending.pop(0))
 
@@ -322,21 +340,24 @@
         ).wait_recv()
         relay(offset)
 
-    for n, offset in enumerate([0] + order):
-        chip = source(offset)
-        ref = arecv.at[chip, 1 - core]
+    for offset in [0] + order:
+        ref = arecv.at[source(offset), 1 - core]
         pltpu.make_async_remote_copy(
             src_ref=ref, dst_ref=ref, send_sem=r_send.at[offset], recv_sem=r_recv.at[offset],
             device_id=mate, device_id_type=MESH,
         ).wait_recv()
+    for chip in range(ny):
         left = jnp.concatenate([arecv[chip, c] for c in range(CORES)], axis=1)
         for b in range(nx):
-            right = jnp.concatenate(
-                [wbuf[b, :, chip * CORES + c].reshape(HD, piece_cols) for c in range(CORES)], axis=0
-            )
             columns = pl.ds(b * piece_cols, piece_cols)
-            term = jnp.dot(left, right, preferred_element_type=jnp.float32)
-            acc[:, columns] = term if n == 0 else acc[:, columns] + term
+            right = []
+            for head in range(chip * CORES, (chip + 1) * CORES):
+                if head < half_heads:
+                    right.append(wlow[:, head, :, columns].reshape(HD, piece_cols))
+                else:
+                    right.append(whigh[b, head - half_heads])
+            term = jnp.dot(left, jnp.concatenate(right, axis=0), preferred_element_type=jnp.float32)
+            acc[:, columns] = term if chip == 0 else acc[:, columns] + term
 
     for c in range(CORES):
         asend_rows = acc[c * drafts:(c + 1) * drafts].astype(jnp.bfloat16)
@@ -353,7 +374,7 @@
     out[:, other] = obuf[2]
     for copy in sends:
         copy.wait_send()
-    for ring in (ring_y, ring_xa, ring_za, ring_zb, ring_xb):
+    for ring in (ring_y, ring_z, ring_x):
         ring.drain()
 
 
@@ -365,8 +386,7 @@
     bf16 = jnp.bfloat16
     dma = pltpu.SemaphoreType.DMA
     vmem = pl.BlockSpec(memory_space=pltpu.VMEM)
-    smem = pl.BlockSpec(memory_space=pltpu.SMEM)
-    hbm = pl.BlockSpec(memory_space=pl.ANY)
+    hbm = pl.BlockSpec(memory_space=pltpu.HBM)
     ring = lambda n: [dma((2, n // 2, 2))] * 2
     out, kept = pl.pallas_call(
         functools.partial(kernel, nx, nz, ny),
@@ -374,11 +394,17 @@
             jax.ShapeDtypeStruct((drafts, width), bf16),
             jax.ShapeDtypeStruct((2, requests, slots, HD), bf16),
         ),
-        in_specs=[vmem, vmem, vmem, smem, smem, hbm, hbm, hbm],
+        in_specs=[hbm] * 8,
         out_specs=(vmem, vmem),
         scratch_shapes=[
+            pltpu.VMEM(hidden.shape, bf16),
+            pltpu.VMEM((1, width), jnp.float32),
+            pltpu.VMEM(w_out.shape, bf16),
+            pltpu.SMEM(cache_len.shape, jnp.int32),
+            pltpu.SMEM((slots, requests), jnp.int32),
             pltpu.VMEM((ny, CORES, 2, drafts // 2, width), bf16),
-            pltpu.VMEM((nx, nz, tp_size, HD // nz, half_width // nx), bf16),
+            pltpu.VMEM((nz, tp_size // 2, HD // nz, half_width), bf16),
+            pltpu.VMEM((nx, tp_size // 2, HD, half_width // nx), bf16),
             pltpu.VMEM((width, 3 * HD), bf16),
             pltpu.VMEM(cache_kv.shape, bf16),
             pltpu.VMEM(ancestors.shape, jnp.int32),
@@ -386,18 +412,18 @@
             pltpu.VMEM((ny, CORES, CORES * drafts, HD), bf16),
             pltpu.VMEM((3, drafts, half_width), bf16),
             pltpu.VMEM((CORES * drafts, half_width), jnp.float32),
-            dma((6,)),
+            dma((11,)),
             dma((tp_size,)),
             dma((tp_size,)),
             *ring(ny),
             dma((2, ny // 2 + 1, 2)),
             dma((2, ny // 2 + 1, 2)),
-            *ring(nx), *ring(nz), *ring(nz), *ring(nx),
+            *ring(nz), *ring(nx),
             dma((ny,)), dma((ny,)), dma((ny,)), dma((ny,)),
             dma, dma,
         ],
         compiler_params=pltpu.CompilerParams(
-            collective_id=0, has_side_effects=True, vmem_limit_bytes=40 * 1024 * 1024
+            collective_id=0, has_side_effects=True, vmem_limit_bytes=62 * 1024 * 1024
         ),
     )(
         hidden, ln_gain.reshape(1, width), w_out, cache_len, accepted.T,

time: 84.7 us -> 77.5 us (0.915)
  the two profiles are of different devices: /device:TPU:1 before, /device:TPU:49 now
where the time goes in v2:
time: 77.5 us; the launch traced here: 77.3 us
  Pallas kernels  73.5 us (95%)
  local copies, waits for them, and re-layouts  3.14 us (4%)
    pallas_call x1, Pallas kernels, on_device(): pl.pallas_call(functools.partial(kernel, nx, nz, ny), out_shape=(jax.Shap...  73.5 us
    unnamed x2, local copies, waits for them, and re-layouts  3.14 us

profile of v2, /device:TPU:49, one launch (start us, length us, event | category | flops | bytes accessed | tf_op | source)
XLA Modules:
  0.0 77.3 jit_solution(7531818682488286372)
XLA Ops:
  0.6 73.5 %shard_map.95 = (bf16[64,2048]{1,0:T(8,128)(2,1)}, bf16[2,16,8,128]{3,2,1,0:T(8,128)(2,1)}) custom-call(bf16[64,2048]{1,0:T(8,128)(2,1)} %hidden_hbm.1, f32[1,2048]{1,0:T(1,128)} %bitcast.4, bf16[128,2048]{1,0:T(8,128)(2,1)} %w_out_hbm.1, s32[16]{0:T(128)} %lens_hbm.1, s32[8,16]{1,0:T(8,128)} %bitcast.5, bf16[3,2048,128]{2,1,0:T(8,128)(2,1)} %bitcast.3, ...), custom_call_target="tpu_custom_call" | custom-call | tf_op jit(solution)/shard_map/pallas_call | solution.py:391
  74.2 1.7 %copy.12 = bf16[64,2048]{1,0:T(8,128)(2,1)} copy(bf16[64,2048]{1,0:T(8,128)(2,1)} %get-tuple-element.4) | data formatting | bytes 524288
  75.8 1.5 %copy.13 = bf16[2,16,8,128]{3,2,1,0:T(8,128)(2,1)} copy(bf16[2,16,8,128]{3,2,1,0:T(8,128)(2,1)} %get-tuple-element.5) | data formatting | bytes 131072

commit v3 on v2

--- a/solution.py
+++ b/solution.py
@@ -276,6 +276,14 @@
             copy.start()
             sends.append(copy)
             order.append(offset)
+            if dist == ring_y.far:
+                copy = pltpu.make_async_remote_copy(
+                    src_ref=asend.at[offset], dst_ref=arecv.at[y, core],
+                    send_sem=r_send.at[offset], recv_sem=r_recv.at[offset],
+                    device_id=(req, owner * CORES + 1 - core), device_id_type=MESH,
+                )
+                copy.start()
+                sends.append(copy)
 
     def source(offset):
         return lax.rem(y + ny - offset, ny) if offset else y
@@ -324,6 +332,8 @@
             pending.insert(0, (0, dist))
         if pending:
             attend(*pending.pop(0))
+        if pending and dist == ring_y.far - 1 and h == 1:
+            attend(*pending.pop(0))
     while pending or along_z or along_x:
         if along_z:
             ring_z.event(along_z.pop(0))
@@ -332,13 +342,14 @@
         if pending:
             attend(*pending.pop(0))
 
-    for offset in order:
+    for offset in sorted(order, key=lambda o: o == ring_y.far):
         ref = arecv.at[source(offset), core]
         pltpu.make_async_remote_copy(
             src_ref=ref, dst_ref=ref, send_sem=a_send.at[offset], recv_sem=a_recv.at[offset],
             device_id=mate, device_id_type=MESH,
         ).wait_recv()
-        relay(offset)
+        if offset != ring_y.far:
+            relay(offset)
 
     for offset in [0] + order:
         ref = arecv.at[source(offset), 1 - core]

time: 77.5 us -> 76.4 us (0.986)
  the two profiles are of different devices: /device:TPU:49 before, /device:TPU:1 now
where the time goes in v3:
time: 76.4 us; the launch traced here: 76.2 us
  Pallas kernels  72.4 us (95%)
  local copies, waits for them, and re-layouts  3.14 us (4%)
    pallas_call x1, Pallas kernels, on_device(): pl.pallas_call(functools.partial(kernel, nx, nz, ny), out_shape=(jax.Shap...  72.4 us
    unnamed x2, local copies, waits for them, and re-layouts  3.14 us

profile of v3, /device:TPU:1, one launch (start us, length us, event | category | flops | bytes accessed | tf_op | source)
XLA Modules:
  0.0 76.2 jit_solution(10713684430210673339)
XLA Ops:
  0.6 72.4 %shard_map.95 = (bf16[64,2048]{1,0:T(8,128)(2,1)}, bf16[2,16,8,128]{3,2,1,0:T(8,128)(2,1)}) custom-call(bf16[64,2048]{1,0:T(8,128)(2,1)} %hidden_hbm.1, f32[1,2048]{1,0:T(1,128)} %bitcast.4, bf16[128,2048]{1,0:T(8,128)(2,1)} %w_out_hbm.1, s32[16]{0:T(128)} %lens_hbm.1, s32[8,16]{1,0:T(8,128)} %bitcast.5, bf16[3,2048,128]{2,1,0:T(8,128)(2,1)} %bitcast.3, ...), custom_call_target="tpu_custom_call" | custom-call | tf_op jit(solution)/shard_map/pallas_call | solution.py:402
  73.1 1.7 %copy.12 = bf16[64,2048]{1,0:T(8,128)(2,1)} copy(bf16[64,2048]{1,0:T(8,128)(2,1)} %get-tuple-element.4) | data formatting | bytes 524288
  74.7 1.5 %copy.13 = bf16[2,16,8,128]{3,2,1,0:T(8,128)(2,1)} copy(bf16[2,16,8,128]{3,2,1,0:T(8,128)(2,1)} %get-tuple-element.5) | data formatting | bytes 131072
